TPU v7x, 32 devices: a whole 2x2x4 slice. The times are simulated.
32 devices in a mesh: groups: 2 (over x), req: 16 (over z, y, core).
Axes of the slice: x: 2, y: 2, z: 4, core: 2. Of those that a mesh axis runs over, the one named last changes fastest.
Arguments:
- queries: bfloat16 [2, 2048, 512], P(None, ('groups', 'req')), parts along dimension 1, may hold values from -40 to 40
- new_kv: bfloat16 [2, 2048, 128], P(None, ('groups', 'req')), parts along dimension 1, may hold values from -4 to 4
- cache: bfloat16 [2, 2048, 128, 128], P(None, ('groups', 'req')), parts along dimension 1, may hold values from -4 to 4
- lengths: int32 [2, 256], P(None, 'groups'), parts along dimension 1, may hold values from 2 to 128
- residual: bfloat16 [2, 256, 2880], P(None, ('groups', 'req')), parts along dimension 1, may hold values from -30 to 30
- o_proj: bfloat16 [4096, 2880], P('req'), may hold values from -1 to 1
- router: bfloat16 [2880, 16], replicated, may hold values from -0.109375 to 0.109375
- w_gate: bfloat16 [64, 2880, 360], P('req'), may hold values from -0.109375 to 0.109375
- w_up: bfloat16 [64, 2880, 360], P('req'), may hold values from -0.109375 to 0.109375
- w_down: bfloat16 [64, 360, 2880], P('req'), may hold values from -0.15625 to 0.15625
- routes: int32 [2, 256, 4], P(None, ('groups', 'req')), parts along dimension 1, may hold values from 0 to 15, all different within a row; in each aligned block of 8 rows (0 to 7, 8 to 15, ..., all dimensions but the last counted through in order) at most 4 rows name the same one
Outputs:
- attended: bfloat16 [2, 256, 2880], P(None, ('groups', 'req')), parts along dimension 1
- layer_out: bfloat16 [2, 256, 2880], P(None, ('groups', 'req')), parts along dimension 1
There are 2 independent parts, one for each index of `groups`. A program takes and returns all parts, laid end to end along the dimension named above; an argument that names none is the same for every part. Nothing has to cross between parts.
Inputs may be any that keep to these rules, and one draw needn't show every extreme that they name: `routes`: each row names 4 different experts; of the 8 rows of one device of one micro-batch at most 4 name any one expert, and in every draw some expert is named by exactly 4 rows of some device.
All inputs are finite; a program needn't handle non-finite values.
Results may differ from a plain program's by a relative error of at most 0.0075.
Values may be sent and summed in bfloat16 or wider, within the bound.
A program may use at most 128 MiB of HBM per device.

v0:
```python
import math
import jax
import jax.numpy as jnp
from jax import lax
from jax.sharding import PartitionSpec as P

D = 2880
HD = 64
KVH = 8
QPK = 8
WIN = 128
EXPERTS = 16
SPLIT = 4
TOPK = 4
MB = 2
REQ_DEV = 8
FFS = 360
CAP = 4


def from_partner(value, axis, stride):
    mask = 2**stride
    pairs = [(source, source ^ mask) for source in range(lax.axis_size(axis))]
    return lax.ppermute(value, axis, pairs)


def attention_rows(query_rows, new_pair, cache_rows, live_count):
    row_total = query_rows.shape[0]
    query_heads = query_rows.reshape(row_total, QPK, HD)
    factor = 1.0 / math.sqrt(HD)
    scores = (
        jnp.einsum(
            "rqd,rpd->rqp", query_heads, cache_rows[:, :, :HD], preferred_element_type=jnp.float32
        )
        * factor
    )
    own_score = (
        jnp.einsum("rqd,rd->rq", query_heads, new_pair[:, :HD], preferred_element_type=jnp.float32)
        * factor
    )
    live = jnp.arange(WIN)[None, None, :] < live_count[:, None, None]
    masked = jnp.where(live, scores, -jnp.inf)
    top_score = jnp.maximum(jnp.max(masked, axis=2), own_score)
    weight_cached = jnp.exp(masked - top_score[:, :, None])
    weight_own = jnp.exp(own_score - top_score)
    total = jnp.sum(weight_cached, axis=2) + weight_own
    prob_cached = (weight_cached / total[:, :, None]).astype(jnp.bfloat16)
    prob_own = (weight_own / total).astype(jnp.bfloat16)
    mixed = jnp.einsum(
        "rqp,rpd->rqd", prob_cached, cache_rows[:, :, HD:], preferred_element_type=jnp.float32
    )
    mixed = (
        mixed
        + prob_own.astype(jnp.float32)[:, :, None]
        * new_pair[:, HD:].astype(jnp.float32)[:, None, :]
    )
    return mixed.astype(jnp.bfloat16)


def bit_value(device_index, bit_number):
    return device_index // (1 << bit_number) % 2


def expert_grouped(buffer, w_gate, w_up, w_down, device_count, device_index):
    batch_width = buffer.shape[0]
    spread = max(1, device_count // EXPERTS)
    experts_local = max(1, EXPERTS // device_count)
    quarters_local = SPLIT // spread
    piece_rows = CAP // spread
    sent = buffer.reshape(batch_width, EXPERTS * spread, piece_rows, D)
    arrived = lax.all_to_all(sent, "req", split_axis=1, concat_axis=2, tiled=True)
    spread_levels = spread.bit_length() - 1
    for section_bit in range(spread_levels):
        upper = bit_value(device_index, section_bit) == 1
        received = from_partner(arrived, "req", section_bit)
        arrived = jnp.where(
            upper,
            jnp.concatenate([received, arrived], axis=2),
            jnp.concatenate([arrived, received], axis=2),
        )
    gate_local = w_gate.reshape(experts_local, quarters_local, D, FFS)
    up_local = w_up.reshape(experts_local, quarters_local, D, FFS)
    down_local = w_down.reshape(experts_local, quarters_local, FFS, D)
    gate_hidden = jnp.einsum(
        "merd,eqdf->meqrf", arrived, gate_local, preferred_element_type=jnp.float32
    )
    up_hidden = jnp.einsum(
        "merd,eqdf->meqrf", arrived, up_local, preferred_element_type=jnp.float32
    )
    active = ((up_hidden + 1.0) * gate_hidden * jax.nn.sigmoid(1.702 * gate_hidden)).astype(
        jnp.bfloat16
    )
    partial_out = jnp.einsum(
        "meqrf,eqfd->merd", active, down_local, preferred_element_type=jnp.float32
    )
    for section_bit in reversed(range(spread_levels)):
        upper = bit_value(device_index, section_bit) == 1
        halves = partial_out.reshape(batch_width, experts_local, 2, partial_out.shape[2] // 2, D)
        keep_part = jnp.where(upper, halves[:, :, 1], halves[:, :, 0])
        send_part = jnp.where(upper, halves[:, :, 0], halves[:, :, 1])
        received = from_partner(send_part.astype(jnp.bfloat16), "req", section_bit).astype(
            send_part.dtype
        )
        partial_out = keep_part + received
    came_back = lax.all_to_all(
        partial_out.astype(jnp.bfloat16), "req", split_axis=2, concat_axis=1, tiled=True
    ).astype(partial_out.dtype)
    return came_back.reshape(batch_width, EXPERTS * CAP, D)


def shards(queries, new_kv, cache, lengths, residual, o_proj, router, w_gate, w_up, w_down, routes):
    device_count = lax.axis_size("req")
    device_index = lax.axis_index("req")
    group_size = device_count // KVH
    group_bits = group_size.bit_length() - 1
    local_rows = queries.shape[1]
    request_count = local_rows * group_size
    block_index = device_index % group_size
    local_lengths = lax.dynamic_slice_in_dim(lengths, block_index * local_rows, local_rows, 1)

    def process_batches(first_batch, batch_width):
        query_part = queries[first_batch : first_batch + batch_width].reshape(
            batch_width * local_rows, QPK * HD
        )
        pair_part = new_kv[first_batch : first_batch + batch_width].reshape(
            batch_width * local_rows, 2 * HD
        )
        cache_part = cache[first_batch : first_batch + batch_width].reshape(
            batch_width * local_rows, WIN, 2 * HD
        )
        live_part = local_lengths[first_batch : first_batch + batch_width].reshape(
            batch_width * local_rows
        )
        mixed = attention_rows(query_part, pair_part, cache_part, live_part)
        held = mixed.reshape(batch_width, local_rows, group_size, QPK // group_size * HD)
        for section_bit in range(group_bits):
            upper = bit_value(device_index, section_bit) == 1
            paired = held.reshape(batch_width, held.shape[1], held.shape[2] // 2, 2, held.shape[3])
            keep_part = jnp.where(upper, paired[:, :, :, 1], paired[:, :, :, 0])
            send_part = jnp.where(upper, paired[:, :, :, 0], paired[:, :, :, 1])
            received = from_partner(send_part, "req", section_bit)
            held = jnp.where(
                upper,
                jnp.concatenate([received, keep_part], axis=1),
                jnp.concatenate([keep_part, received], axis=1),
            )
        head_rows = held.reshape(batch_width, request_count, held.shape[3]).transpose(1, 0, 2)
        summed = lax.psum_scatter(
            jnp.einsum("rmk,kd->rmd", head_rows, o_proj, preferred_element_type=jnp.float32),
            "req",
            scatter_dimension=0,
            tiled=True,
        )
        attended_wide = residual[first_batch : first_batch + batch_width].astype(
            jnp.float32
        ) + summed.transpose(1, 0, 2)
        attended = attended_wide.astype(jnp.bfloat16)
        attended_wide = attended.astype(jnp.float32)
        normed = (
            attended_wide
            * lax.rsqrt(jnp.mean(attended_wide * attended_wide, axis=2, keepdims=True) + 1e-05)
        ).astype(jnp.bfloat16)
        logits = jnp.einsum("mrd,de->mre", normed, router, preferred_element_type=jnp.float32)
        route_ids = routes[first_batch : first_batch + batch_width]
        chosen = jnp.take_along_axis(logits, route_ids, axis=2)
        gates = 1.0 / jnp.sum(jnp.exp(chosen[:, :, None, :] - chosen[:, :, :, None]), axis=3)
        one_hot = (
            route_ids.reshape(batch_width, REQ_DEV * TOPK)[:, :, None]
            == jnp.arange(EXPERTS, dtype=jnp.int32)[None, None, :]
        ).astype(jnp.int32)
        earlier = jnp.cumsum(one_hot, axis=1) - one_hot
        ranks = jnp.sum(earlier * one_hot, axis=2).reshape(batch_width, REQ_DEV, TOPK)
        batch_offset = (jnp.arange(batch_width, dtype=jnp.int32) * (EXPERTS * CAP))[:, None, None]
        flat_index = batch_offset + route_ids * CAP + ranks
        repeated = jnp.repeat(normed.reshape(batch_width * REQ_DEV, D), TOPK, axis=0)
        buffer = (
            jnp.zeros((batch_width * EXPERTS * CAP, D), jnp.bfloat16)
            .at[flat_index.reshape(-1)]
            .set(repeated)
        )
        buffer = buffer.reshape(batch_width, EXPERTS, CAP, D)
        returned = expert_grouped(buffer, w_gate, w_up, w_down, device_count, device_index)
        picked = jnp.take(returned.reshape(batch_width * EXPERTS * CAP, D), flat_index, axis=0)
        mixture = jnp.sum(gates[:, :, :, None] * picked, axis=2)
        layer = (attended_wide + mixture).astype(jnp.bfloat16)
        return (attended, layer)

    results = [process_batches(batch_index, 1) for batch_index in range(MB)]
    attended_all = jnp.concatenate([result[0] for result in results], axis=0)
    layer_all = jnp.concatenate([result[1] for result in results], axis=0)
    return (attended_all, layer_all)


def solution(mesh):
    placed = (
        P(None, ("groups", "req"), None),
        P(None, ("groups", "req"), None),
        P(None, ("groups", "req"), None, None),
        P(None, "groups"),
        P(None, ("groups", "req"), None),
        P("req", None),
        P(),
        P("req", None, None),
        P("req", None, None),
        P("req", None, None),
        P(None, ("groups", "req"), None),
    )
    return jax.shard_map(
        shards,
        mesh=mesh,
        in_specs=placed,
        out_specs=(P(None, ("groups", "req"), None), P(None, ("groups", "req"), None)),
        check_vma=False,
    )
```

profile of v0, /device:TPU:0, one launch (start us, length us, event | category | flops | bytes accessed | tf_op | source)
XLA Modules:
  0.0 243.5 jit_solution(3754402669353376935)
XLA Ops:
  7.2 4.8 %fusion.88 = (bf16[1,64,128,128]{3,2,1,0:T(8,128)(2,1)}, bf16[1,64,128,128]{3,2,1,0:T(8,128)(2,1)}) fusion(bf16[2,64,128,128]{3,2,1,0:T(8,128)(2,1)} %param.17), kind=kLoop, calls=%fused_computation.172 | loop fusion | bytes 8388608 | tf_op jit(solution)/shard_map/slice | solution.py:128
  12.1 4.1 %copy.162 = bf16[1,64,128,128]{2,3,1,0:T(8,128)(2,1)} copy(bf16[1,64,128,128]{3,2,1,0:T(8,128)(2,1)} %get-tuple-element.19) | data formatting | bytes 4194304
  16.8 1.8 fusion.93
  20.5 4.1 %copy.159 = bf16[1,64,128,128]{2,3,1,0:T(8,128)(2,1)} copy(bf16[1,64,128,128]{3,2,1,0:T(8,128)(2,1)} %get-tuple-element.18) | data formatting | bytes 4194304
  25.0 1.8 fusion.94
  29.3 3.1 %copy.132 = f32[128,1,2880]{2,1,0:T(1,128)} copy(f32[128,1,2880]{0,2,1:T(8,128)S(1)} %convolution_bitcast_fusion) | data formatting | bytes 2949120 | tf_op jit(solution)/shard_map/rmk,kd->rmd/dot_general | solution.py:149
  32.9 3.1 %copy.128 = f32[128,1,2880]{2,1,0:T(1,128)} copy(f32[128,1,2880]{0,2,1:T(8,128)S(1)} %convolution_bitcast_fusion.1) | data formatting | bytes 2949120 | tf_op jit(solution)/shard_map/rmk,kd->rmd/dot_general | solution.py:149
  39.3 102.9 %all-reduce.5.cloned.1.call-done = (f32[128,1,2880]{2,1,0:T(1,128)}, f32[128,1,2880]{2,1,0:T(1,128)}) async-done(((f32[128,1,2880]{2,1,0:T(1,128)}, f32[128,1,2880]{2,1,0:T(1,128)}), (f32[128,1,2880]{2,1,0:T(1,128)}, f32[128,1,2880]{2,1,0:T(1,128)})) %all-reduce.5.cloned.1.call-update) | async-done | bytes 2949136
  144.5 1.0 scatter_custom_fusion.1
  146.3 4.1 %all-to-all-start.2 = ((bf16[1,16,4,2880]{3,2,0,1:T(4,128)(2,1)}), bf16[1,16,4,2880]{3,2,0,1:T(4,128)(2,1)S(1)}, u32[]{:S(2)}, u32[]{:S(2)}) async-start(bf16[1,16,4,2880]{3,2,0,1:T(4,128)(2,1)} %reshape.675), calls=%async_computation.2 | async-start | bytes 753664 | tf_op jit(solution)/shard_map/all_to_all | solution.py:71
  155.3 6.9 %all-to-all-done.2 = bf16[1,16,4,2880]{3,2,0,1:T(4,128)(2,1)S(1)} async-done(((bf16[1,16,4,2880]{3,2,0,1:T(4,128)(2,1)}), bf16[1,16,4,2880]{3,2,0,1:T(4,128)(2,1)S(1)}, u32[]{:S(2)}, u32[]{:S(2)}) %all-to-all-start.2) | async-done | bytes 368672 | tf_op jit(solution)/shard_map/all_to_all | solution.py:71
  162.2 3.7 %all-to-all-start = ((bf16[1,16,4,2880]{3,2,0,1:T(4,128)(2,1)}), bf16[1,16,4,2880]{3,2,0,1:T(4,128)(2,1)S(1)}, u32[]{:S(2)}, u32[]{:S(2)}) async-start(bf16[1,16,4,2880]{3,2,0,1:T(4,128)(2,1)} %reshape.668), calls=%async_computation | async-start | bytes 753664 | tf_op jit(solution)/shard_map/all_to_all | solution.py:71
  166.2 6.1 %fusion.98 = f32[64,4,360]{2,0,1:T(8,128)S(1)} fusion(bf16[64,2880,1]{1,0,2:T(8,128)(2,1)S(1)} %reshape.787, bf16[4,2880,360]{1,2,0:T(8,128)(2,1)} %param.22), kind=kOutput, calls=%fused_computation.184 | convolution fusion | flops 530841600 | bytes 9031680 | tf_op jit(solution)/shard_map/merd,eqdf->meqrf/dot_general | solution.py:84
  172.2 9.9 %fusion.2 = bf16[1,1,64,2880]{3,2,0,1:T(8,128)(2,1)S(1)} fusion(bf16[4,360,2880]{2,1,0:T(8,128)(2,1)} %param.24, f32[64,4,360]{2,0,1:T(8,128)S(1)} %fusion.98, bf16[64,2880,1]{1,0,2:T(8,128)(2,1)S(1)} %reshape.787, bf16[4,2880,360]{1,2,0:T(8,128)(2,1)} %param.23), kind=kOutput, calls=%fused_computation.12 | convolution fusion | flops 1062604800 | bytes 17694720 | tf_op jit(solution)/shard_map/meqrf,eqfd->merd/dot_general | solution.py:93
  183.3 3.0 %reduce.8 = bf16[64,2880]{1,0:T(8,128)(2,1)S(1)} reduce(bf16[64,1,1,2880]{3,2,1,0:T(2,128)(2,1)S(1)} %bitcast.159, bf16[]{:T(256)} %broadcast.520), dimensions={1,2}, to_apply=%bitcast.153.reduce_sub_computation | reduce | bytes 737282
  186.3 1.1 reshape.797
  187.4 5.8 %all-to-all-start.3 = ((bf16[16,2,5760]{2,1,0:T(2,128)(2,1)}), bf16[16,2,5760]{2,1,0:T(2,128)(2,1)S(1)}, u32[]{:S(2)}, u32[]{:S(2)}) async-start(bf16[16,2,5760]{2,1,0:T(2,128)(2,1)} %reshape.797), calls=%async_computation.3 | async-start | bytes 737280 | tf_op jit(solution)/shard_map/all_to_all | solution.py:105
  193.4 6.1 %fusion.96 = f32[64,4,360]{2,0,1:T(8,128)S(1)} fusion(bf16[64,2880,1]{1,0,2:T(8,128)(2,1)S(1)} %reshape.785, bf16[4,2880,360]{1,2,0:T(8,128)(2,1)} %param.22), kind=kOutput, calls=%fused_computation.182 | convolution fusion | flops 530841600 | bytes 9031680 | tf_op jit(solution)/shard_map/merd,eqdf->meqrf/dot_general | solution.py:84
  199.5 9.9 %fusion.3 = bf16[1,1,64,2880]{3,2,0,1:T(8,128)(2,1)S(1)} fusion(bf16[4,360,2880]{2,1,0:T(8,128)(2,1)} %param.24, f32[64,4,360]{2,0,1:T(8,128)S(1)} %fusion.96, bf16[64,2880,1]{1,0,2:T(8,128)(2,1)S(1)} %reshape.785, bf16[4,2880,360]{1,2,0:T(8,128)(2,1)} %param.23), kind=kOutput, calls=%fused_computation.13 | convolution fusion | flops 1062604800 | bytes 17694720 | tf_op jit(solution)/shard_map/meqrf,eqfd->merd/dot_general | solution.py:93
  210.0 3.0 %reduce.9 = bf16[64,2880]{1,0:T(8,128)(2,1)S(1)} reduce(bf16[64,1,1,2880]{3,2,1,0:T(2,128)(2,1)S(1)} %bitcast.160, bf16[]{:T(256)} %broadcast.520), dimensions={1,2}, to_apply=%bitcast.154.reduce_sub_computation | reduce | bytes 737282
  213.0 1.1 reshape.799
  214.1 6.0 %all-to-all-start.1 = ((bf16[16,2,5760]{2,1,0:T(2,128)(2,1)}), bf16[16,2,5760]{2,1,0:T(2,128)(2,1)}, u32[]{:S(2)}, u32[]{:S(2)}) async-start(bf16[16,2,5760]{2,1,0:T(2,128)(2,1)} %reshape.799), calls=%async_computation.1 | async-start | bytes 737280 | tf_op jit(solution)/shard_map/all_to_all | solution.py:105
  222.0 10.0 %all-to-all-done.1 = bf16[16,2,5760]{2,1,0:T(2,128)(2,1)} async-done(((bf16[16,2,5760]{2,1,0:T(2,128)(2,1)}), bf16[16,2,5760]{2,1,0:T(2,128)(2,1)}, u32[]{:S(2)}, u32[]{:S(2)}) %all-to-all-start.1) | async-done | bytes 368672 | tf_op jit(solution)/shard_map/all_to_all | solution.py:105
  232.0 2.8 %reshape.800 = bf16[64,1,1,2880]{3,2,1,0:T(2,128)(2,1)S(1)} reshape(bf16[16,2,5760]{2,1,0:T(2,128)(2,1)} %all-to-all-done.1) | data formatting | bytes 737280
  (138 shorter events, 21.9 us)
Async XLA Ops:
  7.2 21.5 %copy-start = (bf16[256,2880]{0,1:T(8,128)(2,1)S(1)}, bf16[256,2880]{0,1:T(8,128)(2,1)}, u32[]{:S(2)}) copy-start(bf16[256,2880]{0,1:T(8,128)(2,1)} %param.20) | copy-start | bytes 4423684
  7.2 135.0 %all-reduce.5.cloned.1.call-start = ((), (), s32[]{:S(2)}) async-start(), calls=%async_computation.4 | async-start | bytes 6029312
  12.1 4.1 %copy-start.4 = (bf16[2,64,512]{2,1,0:T(8,128)(2,1)S(1)}, bf16[2,64,512]{2,1,0:T(8,128)(2,1)}, u32[]{:S(2)}) copy-start(bf16[2,64,512]{2,1,0:T(8,128)(2,1)} %param.15) | copy-start | bytes 393220
  12.1 4.3 %copy-start.8 = (s32[2,128]{1,0:T(2,128)S(1)}, s32[2,128]{1,0:T(2,128)}, u32[]{:S(2)}) copy-start(s32[2,128]{1,0:T(2,128)} %param.18) | copy-start | bytes 3076
  12.1 4.4 %copy-start.7 = (bf16[2,64,128]{2,1,0:T(8,128)(2,1)S(1)}, bf16[2,64,128]{2,1,0:T(8,128)(2,1)}, u32[]{:S(2)}) copy-start(bf16[2,64,128]{2,1,0:T(8,128)(2,1)} %param.16) | copy-start | bytes 98308
  16.4 2.6 %copy-start.1 = (bf16[1,64,128,128]{2,3,1,0:T(8,128)(2,1)S(1)}, bf16[1,64,128,128]{2,3,1,0:T(8,128)(2,1)}, u32[]{:S(2)}) copy-start(bf16[1,64,128,128]{2,3,1,0:T(8,128)(2,1)} %copy.162) | copy-start | bytes 6291460
  20.0 8.7 %collective-permute-start.1 = (bf16[1,64,1,256]{3,1,2,0:T(8,128)(2,1)S(1)}, bf16[1,64,1,256]{3,1,2,0:T(8,128)(2,1)S(1)}, u32[]{:S(2)}, u32[]{:S(2)}) collective-permute-start(bf16[1,64,1,256]{3,1,2,0:T(8,128)(2,1)S(1)} %get-tuple-element.24), channel_id=1, source_target_pairs={{0,1},{1,0},{2,3},{3,2},{4,5},{5,4},{6,7},{7,6},{8,9},{9,8},{10,11... | collective-permute-start | bytes 98312 | tf_op jit(solution)/shard_map/ppermute | solution.py:24
  24.7 2.3 copy-start.2
  26.8 1.4 copy-start.6
  28.1 4.3 %collective-permute-start = (bf16[1,64,1,256]{3,1,2,0:T(8,128)(2,1)S(1)}, bf16[1,64,1,256]{3,1,2,0:T(8,128)(2,1)S(1)}, u32[]{:S(2)}, u32[]{:S(2)}) collective-permute-start(bf16[1,64,1,256]{3,1,2,0:T(8,128)(2,1)S(1)} %get-tuple-element.20), channel_id=1, source_target_pairs={{0,1},{1,0},{2,3},{3,2},{4,5},{5,4},{6,7},{7,6},{8,9},{9,8},{10,11... | collective-permute-start | bytes 98312 | tf_op jit(solution)/shard_map/ppermute | solution.py:24
  36.0 2.0 copy-start.9
  36.0 108.1 %copy-start.5 = (bf16[2,8,2880]{2,1,0:T(8,128)(2,1)S(1)}, bf16[2,8,2880]{2,1,0:T(8,128)(2,1)}, u32[]{:S(2)}) copy-start(bf16[2,8,2880]{2,1,0:T(8,128)(2,1)} %param.19) | copy-start | bytes 276484
  36.0 114.4 %copy-start.3 = (bf16[2880,16]{0,1:T(8,128)(2,1)S(1)}, bf16[2880,16]{0,1:T(8,128)(2,1)}, u32[]{:S(2)}) copy-start(bf16[2880,16]{0,1:T(8,128)(2,1)} %param.21) | copy-start | bytes 276484
  146.3 16.0 %all-to-all-start.2 = ((bf16[1,16,4,2880]{3,2,0,1:T(4,128)(2,1)}), bf16[1,16,4,2880]{3,2,0,1:T(4,128)(2,1)S(1)}, u32[]{:S(2)}, u32[]{:S(2)}) async-start(bf16[1,16,4,2880]{3,2,0,1:T(4,128)(2,1)} %reshape.675), calls=%async_computation.2 | async-start | bytes 753664 | tf_op jit(solution)/shard_map/all_to_all | solution.py:71
  162.2 25.2 %all-to-all-start = ((bf16[1,16,4,2880]{3,2,0,1:T(4,128)(2,1)}), bf16[1,16,4,2880]{3,2,0,1:T(4,128)(2,1)S(1)}, u32[]{:S(2)}, u32[]{:S(2)}) async-start(bf16[1,16,4,2880]{3,2,0,1:T(4,128)(2,1)} %reshape.668), calls=%async_computation | async-start | bytes 753664 | tf_op jit(solution)/shard_map/all_to_all | solution.py:71
  187.4 26.7 %all-to-all-start.3 = ((bf16[16,2,5760]{2,1,0:T(2,128)(2,1)}), bf16[16,2,5760]{2,1,0:T(2,128)(2,1)S(1)}, u32[]{:S(2)}, u32[]{:S(2)}) async-start(bf16[16,2,5760]{2,1,0:T(2,128)(2,1)} %reshape.797), calls=%async_computation.3 | async-start | bytes 737280 | tf_op jit(solution)/shard_map/all_to_all | solution.py:105
  214.1 17.8 %all-to-all-start.1 = ((bf16[16,2,5760]{2,1,0:T(2,128)(2,1)}), bf16[16,2,5760]{2,1,0:T(2,128)(2,1)}, u32[]{:S(2)}, u32[]{:S(2)}) async-start(bf16[16,2,5760]{2,1,0:T(2,128)(2,1)} %reshape.799), calls=%async_computation.1 | async-start | bytes 737280 | tf_op jit(solution)/shard_map/all_to_all | solution.py:105
Sparse Core Ops, SparseCore 0:
  36.1 106.0 all-reduce.4
where the time goes:
time: 244 us
  waiting for transfers between devices  120 us (49%)
  local copies, waits for them, and re-layouts  39.3 us (16%)
  matrix products  38.8 us (16%)
  starting transfers between devices  20.4 us (8%)
  between operations  15.3 us (6%)
  other arithmetic  9.88 us (4%)
    unnamed x2, waiting for transfers between devices  103 us
    dot_general x2, matrix products, expert_grouped(): jnp.einsum('meqrf,eqfd->merd', active, down_local, preferred_element_type...  19.8 us
    unnamed x30, local copies, waits for them, and re-layouts  16.8 us
    dot_general x2, matrix products, expert_grouped(): jnp.einsum('merd,eqdf->meqrf', arrived, gate_local, preferred_element_typ...  12.1 us
    all_to_all x2, starting transfers between devices, expert_grouped(): lax.all_to_all(partial_out.astype(jnp.bfloat16), 'req', split_axis=2, con...  11.8 us
    all_to_all x2, waiting for transfers between devices, expert_grouped(): lax.all_to_all(partial_out.astype(jnp.bfloat16), 'req', split_axis=2, con...  9.97 us
    all_to_all x2, starting transfers between devices, expert_grouped(): lax.all_to_all(sent, 'req', split_axis=1, concat_axis=2, tiled=True)  7.83 us
    all_to_all x2, waiting for transfers between devices, expert_grouped(): lax.all_to_all(sent, 'req', split_axis=1, concat_axis=2, tiled=True)  6.93 us
  transfers between devices with their start and end apart: 7, of which 3 were waited for; matrix products, arithmetic and copies ran while one was open for 26% of the time, Pallas kernels for 0%

commit v1 on v0

--- a/solution.py
+++ b/solution.py
@@ -68,7 +68,15 @@
     quarters_local = SPLIT // spread
     piece_rows = CAP // spread
     sent = buffer.reshape(batch_width, EXPERTS * spread, piece_rows, D)
-    arrived = lax.all_to_all(sent, "req", split_axis=1, concat_axis=2, tiled=True)
+    arrived = jnp.concatenate(
+        jax.lax.all_to_all(
+            jnp.stack(jnp.split(sent, jax.lax.axis_size("req"), axis=1)),
+            "req",
+            split_axis=0,
+            concat_axis=0,
+        ),
+        axis=2,
+    )
     spread_levels = spread.bit_length() - 1
     for section_bit in range(spread_levels):
         upper = bit_value(device_index, section_bit) == 1

time: 244 us -> 258 us (1.057)
  local copies, waits for them, and re-layouts: 39.3 us -> 57.5 us
  waiting for transfers between devices: 120 us -> 113 us
    unnamed x30 -> x60, local copies, waits for them, and re-layouts: 16.8 us -> 35.2 us
    all_to_all x2, waiting for transfers between devices: 6.93 us -> 0.01 us  [expert_grouped(): jax.lax.all_to_all(jnp.stack(jnp.split(sent, jax.lax.axis_size('req'), ax...]
  transfers between devices with their start and end apart: 7 -> 7, of which waited for: 3 -> 2; matrix products, arithmetic and copies ran while one was open for 26% -> 28% of each run, Pallas kernels for 0% -> 0%
where the time goes in v1:
time: 258 us; the launch traced here: 257 us
  waiting for transfers between devices  113 us (44%)
  local copies, waits for them, and re-layouts  57.5 us (22%)
  matrix products  38.8 us (15%)
  starting transfers between devices  22.9 us (9%)
  between operations  15.3 us (6%)
  other arithmetic  9.88 us (4%)
    unnamed x2, waiting for transfers between devices  103 us
    unnamed x60, local copies, waits for them, and re-layouts  35.2 us
    dot_general x2, matrix products, expert_grouped(): jnp.einsum('meqrf,eqfd->merd', active, down_local, preferred_element_type...  19.8 us
    dot_general x2, matrix products, expert_grouped(): jnp.einsum('merd,eqdf->meqrf', arrived, gate_local, preferred_element_typ...  12.1 us
    all_to_all x2, starting transfers between devices, expert_grouped(): lax.all_to_all(partial_out.astype(jnp.bfloat16), 'req', split_axis=2, con...  12.1 us
    all_to_all x2, starting transfers between devices, expert_grouped(): jax.lax.all_to_all(jnp.stack(jnp.split(sent, jax.lax.axis_size('req'), ax...  10.1 us
    all_to_all x2, waiting for transfers between devices, expert_grouped(): lax.all_to_all(partial_out.astype(jnp.bfloat16), 'req', split_axis=2, con...  9.97 us
    dot_general x2, local copies, waits for them, and re-layouts, process_batches(): jnp.einsum('rmk,kd->rmd', head_rows, o_proj, preferred_element_type=jnp.f...  6.17 us
  transfers between devices with their start and end apart: 7, of which 2 were waited for; matrix products, arithmetic and copies ran while one was open for 28% of the time, Pallas kernels for 0%

profile of v1, /device:TPU:0, one launch (start us, length us, event | category | flops | bytes accessed | tf_op | source)
XLA Modules:
  0.0 257.2 jit_solution(4087532599490681514)
XLA Ops:
  7.2 4.8 %fusion.88 = (bf16[1,64,128,128]{3,2,1,0:T(8,128)(2,1)}, bf16[1,64,128,128]{3,2,1,0:T(8,128)(2,1)}) fusion(bf16[2,64,128,128]{3,2,1,0:T(8,128)(2,1)} %param.17), kind=kLoop, calls=%fused_computation.236 | loop fusion | bytes 8388608 | tf_op jit(solution)/shard_map/slice | solution.py:136
  12.1 4.1 %copy.222 = bf16[1,64,128,128]{2,3,1,0:T(8,128)(2,1)} copy(bf16[1,64,128,128]{3,2,1,0:T(8,128)(2,1)} %get-tuple-element.19) | data formatting | bytes 4194304
  16.8 1.8 fusion.93
  20.5 4.1 %copy.219 = bf16[1,64,128,128]{2,3,1,0:T(8,128)(2,1)} copy(bf16[1,64,128,128]{3,2,1,0:T(8,128)(2,1)} %get-tuple-element.18) | data formatting | bytes 4194304
  25.0 1.8 fusion.94
  29.3 3.1 %copy.192 = f32[128,1,2880]{2,1,0:T(1,128)} copy(f32[128,1,2880]{0,2,1:T(8,128)S(1)} %convolution_bitcast_fusion) | data formatting | bytes 2949120 | tf_op jit(solution)/shard_map/rmk,kd->rmd/dot_general | solution.py:157
  32.9 3.1 %copy.188 = f32[128,1,2880]{2,1,0:T(1,128)} copy(f32[128,1,2880]{0,2,1:T(8,128)S(1)} %convolution_bitcast_fusion.1) | data formatting | bytes 2949120 | tf_op jit(solution)/shard_map/rmk,kd->rmd/dot_general | solution.py:157
  39.3 102.9 %all-reduce.5.cloned.1.call-done = (f32[128,1,2880]{2,1,0:T(1,128)}, f32[128,1,2880]{2,1,0:T(1,128)}) async-done(((f32[128,1,2880]{2,1,0:T(1,128)}, f32[128,1,2880]{2,1,0:T(1,128)}), (f32[128,1,2880]{2,1,0:T(1,128)}, f32[128,1,2880]{2,1,0:T(1,128)})) %all-reduce.5.cloned.1.call-update) | async-done | bytes 2949136
  145.1 1.0 scatter_custom_fusion.1
  156.0 4.1 %all-to-all-start.2 = ((bf16[16,1,1,4,2880]{4,3,2,1,0:T(4,128)(2,1)}), bf16[16,1,1,4,2880]{4,3,2,1,0:T(4,128)(2,1)S(1)}, u32[]{:S(2)}, u32[]{:S(2)}) async-start(bf16[16,1,1,4,2880]{4,3,2,1,0:T(4,128)(2,1)} %constant_dynamic-update-slice_fusion.16), calls=%async_computation.2 | async-start | bytes 753664 | tf_op jit(solution)/shard_map/all_to_all | solution.py:72
  162.4 1.0 scatter_custom_fusion
  173.5 6.0 %all-to-all-start = ((bf16[16,1,1,4,2880]{4,3,2,1,0:T(4,128)(2,1)}), bf16[16,1,1,4,2880]{4,3,2,1,0:T(4,128)(2,1)S(1)}, u32[]{:S(2)}, u32[]{:S(2)}) async-start(bf16[16,1,1,4,2880]{4,3,2,1,0:T(4,128)(2,1)} %constant_dynamic-update-slice_fusion), calls=%async_computation | async-start | bytes 753664 | tf_op jit(solution)/shard_map/all_to_all | solution.py:72
  179.7 6.1 %fusion.98 = f32[64,4,360]{2,0,1:T(8,128)S(1)} fusion(bf16[64,2880,1]{1,0,2:T(8,128)(2,1)S(1)} %reshape.783, bf16[4,2880,360]{1,2,0:T(8,128)(2,1)} %param.22), kind=kOutput, calls=%fused_computation.248 | convolution fusion | flops 530841600 | bytes 9031680 | tf_op jit(solution)/shard_map/merd,eqdf->meqrf/dot_general | solution.py:92
  185.7 9.9 %fusion.2 = bf16[1,1,64,2880]{3,2,0,1:T(8,128)(2,1)S(1)} fusion(bf16[4,360,2880]{2,1,0:T(8,128)(2,1)} %param.24, f32[64,4,360]{2,0,1:T(8,128)S(1)} %fusion.98, bf16[64,2880,1]{1,0,2:T(8,128)(2,1)S(1)} %reshape.783, bf16[4,2880,360]{1,2,0:T(8,128)(2,1)} %param.23), kind=kOutput, calls=%fused_computation.12 | convolution fusion | flops 1062604800 | bytes 17694720 | tf_op jit(solution)/shard_map/meqrf,eqfd->merd/dot_general | solution.py:101
  196.8 3.0 %reduce.8 = bf16[64,2880]{1,0:T(8,128)(2,1)S(1)} reduce(bf16[64,1,1,2880]{3,2,1,0:T(2,128)(2,1)S(1)} %bitcast.283, bf16[]{:T(256)} %broadcast.520), dimensions={1,2}, to_apply=%bitcast.277.reduce_sub_computation | reduce | bytes 737282
  199.8 1.1 reshape.793
  200.9 6.0 %all-to-all-start.3 = ((bf16[16,2,5760]{2,1,0:T(2,128)(2,1)}), bf16[16,2,5760]{2,1,0:T(2,128)(2,1)S(1)}, u32[]{:S(2)}, u32[]{:S(2)}) async-start(bf16[16,2,5760]{2,1,0:T(2,128)(2,1)} %reshape.793), calls=%async_computation.3 | async-start | bytes 737280 | tf_op jit(solution)/shard_map/all_to_all | solution.py:113
  207.1 6.1 %fusion.96 = f32[64,4,360]{2,0,1:T(8,128)S(1)} fusion(bf16[64,2880,1]{1,0,2:T(8,128)(2,1)S(1)} %reshape.781, bf16[4,2880,360]{1,2,0:T(8,128)(2,1)} %param.22), kind=kOutput, calls=%fused_computation.246 | convolution fusion | flops 530841600 | bytes 9031680 | tf_op jit(solution)/shard_map/merd,eqdf->meqrf/dot_general | solution.py:92
  213.2 9.9 %fusion.3 = bf16[1,1,64,2880]{3,2,0,1:T(8,128)(2,1)S(1)} fusion(bf16[4,360,2880]{2,1,0:T(8,128)(2,1)} %param.24, f32[64,4,360]{2,0,1:T(8,128)S(1)} %fusion.96, bf16[64,2880,1]{1,0,2:T(8,128)(2,1)S(1)} %reshape.781, bf16[4,2880,360]{1,2,0:T(8,128)(2,1)} %param.23), kind=kOutput, calls=%fused_computation.13 | convolution fusion | flops 1062604800 | bytes 17694720 | tf_op jit(solution)/shard_map/meqrf,eqfd->merd/dot_general | solution.py:101
  223.7 3.0 %reduce.9 = bf16[64,2880]{1,0:T(8,128)(2,1)S(1)} reduce(bf16[64,1,1,2880]{3,2,1,0:T(2,128)(2,1)S(1)} %bitcast.284, bf16[]{:T(256)} %broadcast.520), dimensions={1,2}, to_apply=%bitcast.278.reduce_sub_computation | reduce | bytes 737282
  226.7 1.1 reshape.795
  227.8 6.0 %all-to-all-start.1 = ((bf16[16,2,5760]{2,1,0:T(2,128)(2,1)}), bf16[16,2,5760]{2,1,0:T(2,128)(2,1)}, u32[]{:S(2)}, u32[]{:S(2)}) async-start(bf16[16,2,5760]{2,1,0:T(2,128)(2,1)} %reshape.795), calls=%async_computation.1 | async-start | bytes 737280 | tf_op jit(solution)/shard_map/all_to_all | solution.py:113
  235.7 10.0 %all-to-all-done.1 = bf16[16,2,5760]{2,1,0:T(2,128)(2,1)} async-done(((bf16[16,2,5760]{2,1,0:T(2,128)(2,1)}), bf16[16,2,5760]{2,1,0:T(2,128)(2,1)}, u32[]{:S(2)}, u32[]{:S(2)}) %all-to-all-start.1) | async-done | bytes 368672 | tf_op jit(solution)/shard_map/all_to_all | solution.py:113
  245.7 2.8 %reshape.796 = bf16[64,1,1,2880]{3,2,1,0:T(2,128)(2,1)S(1)} reshape(bf16[16,2,5760]{2,1,0:T(2,128)(2,1)} %all-to-all-done.1) | data formatting | bytes 737280
  (170 shorter events, 39.1 us)
Async XLA Ops:
  7.2 21.5 %copy-start = (bf16[256,2880]{0,1:T(8,128)(2,1)S(1)}, bf16[256,2880]{0,1:T(8,128)(2,1)}, u32[]{:S(2)}) copy-start(bf16[256,2880]{0,1:T(8,128)(2,1)} %param.20) | copy-start | bytes 4423684
  7.2 135.0 %all-reduce.5.cloned.1.call-start = ((), (), s32[]{:S(2)}) async-start(), calls=%async_computation.4 | async-start | bytes 6029312
  12.1 4.1 %copy-start.4 = (bf16[2,64,512]{2,1,0:T(8,128)(2,1)S(1)}, bf16[2,64,512]{2,1,0:T(8,128)(2,1)}, u32[]{:S(2)}) copy-start(bf16[2,64,512]{2,1,0:T(8,128)(2,1)} %param.15) | copy-start | bytes 393220
  12.1 4.3 %copy-start.8 = (s32[2,128]{1,0:T(2,128)S(1)}, s32[2,128]{1,0:T(2,128)}, u32[]{:S(2)}) copy-start(s32[2,128]{1,0:T(2,128)} %param.18) | copy-start | bytes 3076
  12.1 4.4 %copy-start.7 = (bf16[2,64,128]{2,1,0:T(8,128)(2,1)S(1)}, bf16[2,64,128]{2,1,0:T(8,128)(2,1)}, u32[]{:S(2)}) copy-start(bf16[2,64,128]{2,1,0:T(8,128)(2,1)} %param.16) | copy-start | bytes 98308
  16.4 2.6 %copy-start.1 = (bf16[1,64,128,128]{2,3,1,0:T(8,128)(2,1)S(1)}, bf16[1,64,128,128]{2,3,1,0:T(8,128)(2,1)}, u32[]{:S(2)}) copy-start(bf16[1,64,128,128]{2,3,1,0:T(8,128)(2,1)} %copy.222) | copy-start | bytes 6291460
  20.0 8.7 %collective-permute-start.1 = (bf16[1,64,1,256]{3,1,2,0:T(8,128)(2,1)S(1)}, bf16[1,64,1,256]{3,1,2,0:T(8,128)(2,1)S(1)}, u32[]{:S(2)}, u32[]{:S(2)}) collective-permute-start(bf16[1,64,1,256]{3,1,2,0:T(8,128)(2,1)S(1)} %get-tuple-element.24), channel_id=1, source_target_pairs={{0,1},{1,0},{2,3},{3,2},{4,5},{5,4},{6,7},{7,6},{8,9},{9,8},{10,11... | collective-permute-start | bytes 98312 | tf_op jit(solution)/shard_map/ppermute | solution.py:24
  24.7 2.3 copy-start.2
  26.8 1.4 copy-start.6
  28.1 4.3 %collective-permute-start = (bf16[1,64,1,256]{3,1,2,0:T(8,128)(2,1)S(1)}, bf16[1,64,1,256]{3,1,2,0:T(8,128)(2,1)S(1)}, u32[]{:S(2)}, u32[]{:S(2)}) collective-permute-start(bf16[1,64,1,256]{3,1,2,0:T(8,128)(2,1)S(1)} %get-tuple-element.20), channel_id=1, source_target_pairs={{0,1},{1,0},{2,3},{3,2},{4,5},{5,4},{6,7},{7,6},{8,9},{9,8},{10,11... | collective-permute-start | bytes 98312 | tf_op jit(solution)/shard_map/ppermute | solution.py:24
  36.0 2.0 copy-start.9
  36.0 108.1 %copy-start.5 = (bf16[2,8,2880]{2,1,0:T(8,128)(2,1)S(1)}, bf16[2,8,2880]{2,1,0:T(8,128)(2,1)}, u32[]{:S(2)}) copy-start(bf16[2,8,2880]{2,1,0:T(8,128)(2,1)} %param.19) | copy-start | bytes 276484
  143.1 17.1 %copy-start.3 = (bf16[2880,16]{0,1:T(8,128)(2,1)S(1)}, bf16[2880,16]{0,1:T(8,128)(2,1)}, u32[]{:S(2)}) copy-start(bf16[2880,16]{0,1:T(8,128)(2,1)} %param.21) | copy-start | bytes 276484
  156.0 17.5 %all-to-all-start.2 = ((bf16[16,1,1,4,2880]{4,3,2,1,0:T(4,128)(2,1)}), bf16[16,1,1,4,2880]{4,3,2,1,0:T(4,128)(2,1)S(1)}, u32[]{:S(2)}, u32[]{:S(2)}) async-start(bf16[16,1,1,4,2880]{4,3,2,1,0:T(4,128)(2,1)} %constant_dynamic-update-slice_fusion.16), calls=%async_computation.2 | async-start | bytes 753664 | tf_op jit(solution)/shard_map/all_to_all | solution.py:72
  173.5 27.4 %all-to-all-start = ((bf16[16,1,1,4,2880]{4,3,2,1,0:T(4,128)(2,1)}), bf16[16,1,1,4,2880]{4,3,2,1,0:T(4,128)(2,1)S(1)}, u32[]{:S(2)}, u32[]{:S(2)}) async-start(bf16[16,1,1,4,2880]{4,3,2,1,0:T(4,128)(2,1)} %constant_dynamic-update-slice_fusion), calls=%async_computation | async-start | bytes 753664 | tf_op jit(solution)/shard_map/all_to_all | solution.py:72
  200.9 26.9 %all-to-all-start.3 = ((bf16[16,2,5760]{2,1,0:T(2,128)(2,1)}), bf16[16,2,5760]{2,1,0:T(2,128)(2,1)S(1)}, u32[]{:S(2)}, u32[]{:S(2)}) async-start(bf16[16,2,5760]{2,1,0:T(2,128)(2,1)} %reshape.793), calls=%async_computation.3 | async-start | bytes 737280 | tf_op jit(solution)/shard_map/all_to_all | solution.py:113
  227.8 17.8 %all-to-all-start.1 = ((bf16[16,2,5760]{2,1,0:T(2,128)(2,1)}), bf16[16,2,5760]{2,1,0:T(2,128)(2,1)}, u32[]{:S(2)}, u32[]{:S(2)}) async-start(bf16[16,2,5760]{2,1,0:T(2,128)(2,1)} %reshape.795), calls=%async_computation.1 | async-start | bytes 737280 | tf_op jit(solution)/shard_map/all_to_all | solution.py:113
Sparse Core Ops, SparseCore 0:
  36.1 106.0 all-reduce.4
